TPU v7x, 128 devices: a whole 4x4x4 slice. The times are simulated.
128 devices in a mesh: shard: 16 (over z, x), context: 4 (over y), tensor: 2 (over core).
Axes of the slice: x: 4, y: 4, z: 4, core: 2. Of those that a mesh axis runs over, the one named last changes fastest.
Arguments:
- inputs: float32 [32, 512, 768], P('shard', 'context'), may hold values from -6 to 6
- segment_ids: int32 [32, 512], P('shard', 'context'), may hold values from 0 to 3, never falling along the last dimension, each value on 1 to 256 neighbouring positions
- projection: bfloat16 [2, 3, 768, 768], P(None, None, 'shard', 'tensor'), may hold values from -1 to 1
- head_bias: bfloat16 [2, 2, 12, 64], P(None, None, 'tensor', 'shard'), may hold values from -3 to 3
- mixing: bfloat16 [2, 768, 768], P(None, 'tensor', 'shard'), may hold values from -0.875 to 0.875
- expansion: bfloat16 [2, 768, 3072], P(None, 'shard', 'tensor'), may hold values from -0.21875 to 0.21875
- hidden_bias: bfloat16 [2, 48, 64], P(None, 'tensor', 'shard'), may hold values from -3 to 3
- contraction: bfloat16 [2, 3072, 768], P(None, 'tensor', 'shard'), may hold values from -0.109375 to 0.109375
- norm_gains: bfloat16 [2, 2, 768], P(None, None, 'shard'), may hold values from 0.3984375 to 1.59375
- offsets: bfloat16 [2, 4, 768], P(None, None, 'shard'), may hold values from -2 to 2
- cotangent: float32 [32, 512, 768], P('shard', 'context'), may hold values from -6 to 6
Outputs:
- outputs: float32 [32, 512, 768], P('shard', 'context')
- input_grad: float32 [32, 512, 768], P('shard', 'context')
- grad_projection: float32 [2, 3, 768, 768], P(None, None, 'shard', 'tensor')
- head_grad: float32 [2, 2, 12, 64], P(None, None, 'tensor', 'shard')
- grad_mixing: float32 [2, 768, 768], P(None, 'tensor', 'shard')
- grad_expansion: float32 [2, 768, 3072], P(None, 'shard', 'tensor')
- hidden_grad: float32 [2, 48, 64], P(None, 'tensor', 'shard')
- grad_contraction: float32 [2, 3072, 768], P(None, 'tensor', 'shard')
- gains_grad: float32 [2, 2, 768], P(None, None, 'shard')
- grad_offsets: float32 [2, 4, 768], P(None, None, 'shard')
Inputs may be any that keep to these rules, and one draw needn't show every extreme that they name: `segment_ids`: within a row ids never fall; every document holds 1 to 256 positions and in every row some document holds exactly 256.
All inputs are finite; a program needn't handle non-finite values.
Results may differ from a plain program's by a relative error of at most 0.033.
Values may be sent and summed in bfloat16 or wider, within the bound.
No kernel may reach another device: no remote copies, remote signals or barrier semaphores. Data moves between devices by JAX's collectives and lax.ppermute only.
A program may use at most 128 MiB of HBM per device.

v0:
```python
import jax
import jax.numpy as jnp
from jax import lax
from jax.sharding import PartitionSpec as P

HEAD = 64
EPS = 1e-05
GELU_COEF = 0.7978845608028654
GELU_CUBE = 0.044715
MASKED = -1e30
HALF = jnp.bfloat16
FULL = jnp.float32


def gelu_value(preact):
    inner_arg = GELU_COEF * (preact + GELU_CUBE * preact * preact * preact)
    return 0.5 * preact * (1.0 + jnp.tanh(inner_arg))


def gelu_slope(preact):
    inner_arg = GELU_COEF * (preact + GELU_CUBE * preact * preact * preact)
    tanh_value = jnp.tanh(inner_arg)
    return 0.5 * (1.0 + tanh_value) + 0.5 * preact * (1.0 - tanh_value * tanh_value) * GELU_COEF * (
        1.0 + 3.0 * GELU_CUBE * preact * preact
    )


def norm_forward(stream):
    center = stream - jnp.mean(stream, axis=-1, keepdims=True)
    spread = lax.rsqrt(jnp.mean(center * center, axis=-1, keepdims=True) + EPS)
    return (center * spread, spread)


def norm_backward(upstream, normed, spread, gain_row):
    scaled = upstream * gain_row
    first_mean = jnp.mean(scaled, axis=-1, keepdims=True)
    second_mean = jnp.mean(scaled * normed, axis=-1, keepdims=True)
    return spread * (scaled - first_mean - normed * second_mean)


def dot(left, right, left_dim, right_dim):
    return lax.dot_general(
        left, right, (((left_dim,), (right_dim,)), ((), ())), preferred_element_type=FULL
    )


def pair_sum(part):
    size = lax.axis_size("tensor")
    other = lax.ppermute(part, "tensor", [(i, (i + 1) % size) for i in range(size)])
    return part.astype(FULL) + other.astype(FULL)


def from_before(block, steps):
    size = lax.axis_size("context")
    return lax.ppermute(block, "context", [(i, i + steps) for i in range(size - steps)])


def from_after(block, steps):
    size = lax.axis_size("context")
    return lax.ppermute(block, "context", [(i + steps, i) for i in range(size - steps)])


def context_sum(part):
    size = lax.axis_size("context")
    total = part.astype(FULL)
    for steps in range(1, size):
        moved = lax.ppermute(part, "context", [(i, (i + steps) % size) for i in range(size)])
        total = total + moved.astype(FULL)
    return total


def masked_scores(query_block, key_block, visible, head_scale):
    scores = (
        jnp.einsum("rqhe,rkhe->rhqk", query_block, key_block, preferred_element_type=FULL)
        * head_scale
    )
    return jnp.where(visible, scores, MASKED)


def per_device(
    inputs,
    segment_ids,
    projection,
    head_bias,
    mixing,
    expansion,
    hidden_bias,
    contraction,
    norm_gains,
    offsets,
    cotangent,
):
    layers = projection.shape[0]
    rows, block, width = inputs.shape
    shards = lax.axis_size("shard")
    contexts = lax.axis_size("context")
    own = projection.shape[2]
    heads = head_bias.shape[2]
    head_cols = projection.shape[3]
    hidden = expansion.shape[2]
    tokens = rows * block
    head_scale = HEAD ** (-0.5)
    back_steps = 2
    gathered = []
    for layer in range(layers):
        packed = jnp.concatenate(
            [
                projection[layer, 0],
                projection[layer, 1],
                projection[layer, 2],
                mixing[layer].T,
                expansion[layer],
                contraction[layer].T,
            ],
            axis=1,
        )
        gathered.append(lax.all_gather(packed, "shard", axis=0, tiled=True))
    small_parts = [norm_gains, offsets, head_bias, hidden_bias]
    small_sizes = [part.size for part in small_parts]
    small_total = sum(small_sizes)
    small_padded = -(-small_total // 1024) * 1024
    small = jnp.concatenate(
        [part.reshape(-1) for part in small_parts]
        + [jnp.zeros((small_padded - small_total,), HALF)]
    )
    small = jnp.broadcast_to(small.reshape(1, -1, 128), (shards, small_padded // 128, 128))
    small = lax.all_to_all(small, "shard", 0, 0).reshape(shards, small_padded)

    def widen(index):
        start = sum(small_sizes[:index])
        shape = small_parts[index].shape
        piece = small[:, start : start + small_sizes[index]].astype(FULL).reshape((shards,) + shape)
        piece = jnp.moveaxis(piece, 0, -2)
        return piece.reshape(shape[:-1] + (shards * shape[-1],))

    gains_all, offsets_all = (widen(0), widen(1))
    head_all = widen(2).reshape(layers, 2, head_cols)
    hidden_all = widen(3).reshape(layers, hidden)
    seg_before = [from_before(segment_ids, steps) for steps in range(back_steps, 0, -1)]
    segments_all = jnp.concatenate(seg_before + [segment_ids], axis=1)
    query_pos = jnp.arange(block, dtype=jnp.int32) + back_steps * block
    key_pos = jnp.arange((back_steps + 1) * block, dtype=jnp.int32)
    first_key = (back_steps - lax.axis_index("context")) * block
    visible = (
        (segments_all[:, None, :] == segment_ids[:, :, None])
        & (key_pos[None, None, :] <= query_pos[None, :, None])
        & (key_pos >= first_key)[None, None, :]
    )
    visible = visible[:, None]

    def split_weights(weights):
        ends = [3 * head_cols, 4 * head_cols, 4 * head_cols + hidden, 4 * head_cols + 2 * hidden]
        return (
            weights[:, : ends[0]],
            weights[:, ends[0] : ends[1]],
            weights[:, ends[1] : ends[2]],
            weights[:, ends[2] : ends[3]],
        )

    stream = inputs.reshape(tokens, width)
    kept = []
    for layer in range(layers):
        qkv_weight, out_weight, up_weight, down_weight = split_weights(gathered[layer])
        gain, offset = (gains_all[layer], offsets_all[layer])
        normed_one, spread_one = norm_forward(stream)
        attend_input = (normed_one * gain[0] + offset[0]).astype(HALF)
        zero_bias = jnp.zeros((head_cols,), FULL)
        bias = jnp.concatenate([head_all[layer, 0], zero_bias, head_all[layer, 1]])
        projected = (dot(attend_input, qkv_weight, 1, 0) + bias).astype(HALF)
        query_rows = projected[:, :head_cols]
        key_value = projected[:, head_cols:].reshape(rows, block, 2 * head_cols)
        before = [from_before(key_value, steps) for steps in range(back_steps, 0, -1)]
        key_value_all = jnp.concatenate(before + [key_value], axis=1)
        query_block = query_rows.reshape(rows, block, heads, HEAD)
        key_block = key_value_all[:, :, :head_cols].reshape(rows, -1, heads, HEAD)
        value_block = key_value_all[:, :, head_cols:].reshape(rows, -1, heads, HEAD)
        masked = masked_scores(query_block, key_block, visible, head_scale)
        row_top = jnp.max(masked, axis=-1, keepdims=True)
        log_total = row_top + jnp.log(jnp.sum(jnp.exp(masked - row_top), axis=-1, keepdims=True))
        soft_half = jnp.exp(masked - log_total).astype(HALF)
        attended = (
            jnp.einsum("rhqk,rkhe->rqhe", soft_half, value_block, preferred_element_type=FULL)
            .astype(HALF)
            .reshape(tokens, head_cols)
        )
        middle = stream + pair_sum(dot(attended, out_weight, 1, 1)) + offset[2]
        normed_two, spread_two = norm_forward(middle)
        feed_input = (normed_two * gain[1] + offset[1]).astype(HALF)
        preact = dot(feed_input, up_weight, 1, 0) + hidden_all[layer]
        activation = gelu_value(preact).astype(HALF)
        stream = middle + pair_sum(dot(activation, down_weight, 1, 1)) + offset[3]
        kept.append(
            (
                normed_one,
                spread_one,
                attend_input,
                query_block,
                key_block,
                value_block,
                log_total,
                attended,
                normed_two,
                spread_two,
                feed_input,
                preact,
                activation,
            )
        )

    def scatter(parts):
        packed = jnp.concatenate([part.astype(HALF) for part in parts], axis=1)
        return lax.psum_scatter(packed, "shard", scatter_dimension=0, tiled=True)

    upstream = cotangent.reshape(tokens, width)
    feed_shares, attend_shares, vectors = ([None] * layers, [None] * layers, [None] * layers)
    for layer in reversed(range(layers)):
        (
            normed_one,
            spread_one,
            attend_input,
            query_block,
            key_block,
            value_block,
            log_total,
            attended,
            normed_two,
            spread_two,
            feed_input,
            preact,
            activation,
        ) = kept[layer]
        qkv_weight, out_weight, up_weight, down_weight = split_weights(gathered[layer])
        gain = gains_all[layer]
        upstream_half = upstream.astype(HALF)
        contraction_part = dot(upstream_half, activation, 0, 0)
        offset_down = jnp.sum(upstream, axis=0)
        hidden_back = dot(upstream_half, down_weight, 1, 0) * gelu_slope(preact)
        hidden_half = hidden_back.astype(HALF)
        hidden_part = jnp.sum(hidden_back, axis=0)
        expansion_part = dot(feed_input, hidden_half, 0, 0)
        feed_shares[layer] = scatter([expansion_part, contraction_part])
        feed_back = pair_sum(dot(hidden_half, up_weight, 1, 1).astype(HALF))
        gain_two = jnp.sum(feed_back * normed_two, axis=0)
        offset_two = jnp.sum(feed_back, axis=0)
        middle_back = upstream + norm_backward(feed_back, normed_two, spread_two, gain[1])
        middle_half = middle_back.astype(HALF)
        mixing_part = dot(middle_half, attended, 0, 0)
        offset_mix = jnp.sum(middle_back, axis=0)
        attended_back = dot(middle_half, out_weight, 1, 0).astype(HALF)
        back_heads = attended_back.reshape(rows, block, heads, HEAD)
        attended_heads = attended.reshape(rows, block, heads, HEAD)
        row_delta = jnp.sum(back_heads.astype(FULL) * attended_heads.astype(FULL), axis=-1)
        masked = masked_scores(query_block, key_block, visible, head_scale)
        soft = jnp.exp(masked - log_total)
        soft_half = soft.astype(HALF)
        prob_back = jnp.einsum(
            "rqhe,rkhe->rhqk", back_heads, value_block, preferred_element_type=FULL
        )
        score_back = (
            soft * (prob_back - jnp.transpose(row_delta, (0, 2, 1))[..., None]) * head_scale
        ).astype(HALF)
        query_back = jnp.einsum(
            "rhqk,rkhe->rqhe", score_back, key_block, preferred_element_type=FULL
        ).reshape(tokens, head_cols)
        key_full = jnp.einsum(
            "rhqk,rqhe->rkhe", score_back, query_block, preferred_element_type=FULL
        ).reshape(rows, -1, head_cols)
        value_full = jnp.einsum(
            "rhqk,rqhe->rkhe", soft_half, back_heads, preferred_element_type=FULL
        ).reshape(rows, -1, head_cols)
        both_full = jnp.concatenate([key_full, value_full], axis=2)
        both_back = both_full[:, back_steps * block :]
        for steps in range(1, back_steps + 1):
            start = (back_steps - steps) * block
            both_back = both_back + from_after(
                both_full[:, start : start + block].astype(HALF), steps
            ).astype(FULL)
        both_back = both_back.reshape(tokens, 2 * head_cols)
        head_part = jnp.concatenate(
            [jnp.sum(query_back, axis=0), jnp.sum(both_back[:, head_cols:], axis=0)]
        )
        project_back = jnp.concatenate([query_back, both_back], axis=1).astype(HALF)
        projection_part = dot(attend_input, project_back, 0, 0)
        attend_shares[layer] = scatter([projection_part, mixing_part])
        input_back = pair_sum(dot(project_back, qkv_weight, 1, 1).astype(HALF))
        gain_one = jnp.sum(input_back * normed_one, axis=0)
        offset_one = jnp.sum(input_back, axis=0)
        upstream = middle_back + norm_backward(input_back, normed_one, spread_one, gain[0])
        vectors[layer] = (
            [gain_one, gain_two],
            [offset_one, offset_two, offset_mix, offset_down],
            head_part,
            hidden_part,
        )

    def spread_out(values, shape):
        lead = shape[:-1]
        values = values.reshape(lead + (shards, shape[-1]))
        return jnp.moveaxis(values, -2, 0).reshape(shards, -1)

    gain_sums = jnp.stack([jnp.stack(entry[0]) for entry in vectors])
    offset_sums = jnp.stack([jnp.stack(entry[1]) for entry in vectors])
    head_sums = jnp.stack([entry[2] for entry in vectors])
    hidden_sums = jnp.stack([entry[3] for entry in vectors])
    vector_pack = jnp.concatenate(
        [
            spread_out(values, part.shape)
            for values, part in zip((gain_sums, offset_sums, head_sums, hidden_sums), small_parts)
        ]
        + [jnp.zeros((shards, small_padded - small_total), FULL)],
        axis=1,
    )
    vector_pack = lax.all_to_all(vector_pack.reshape(shards, -1, 128), "shard", 0, 0)
    vector_own = context_sum(jnp.sum(vector_pack, axis=0)).reshape(-1)
    vector_out = []
    for index, part in enumerate(small_parts):
        start = sum(small_sizes[:index])
        vector_out.append(vector_own[start : start + small_sizes[index]].reshape(part.shape))
    gains_grad, offsets_grad, head_grad, hidden_grad = vector_out
    feed_own = [context_sum(share) for share in feed_shares]
    attend_own = [context_sum(share) for share in attend_shares]
    projection_grad = jnp.stack(
        [
            jnp.stack([share[:, k * head_cols : (k + 1) * head_cols] for k in range(3)])
            for share in attend_own
        ]
    )
    mixing_grad = jnp.stack([share[:, 3 * head_cols :].T for share in attend_own])
    expansion_grad = jnp.stack([share[:, :hidden] for share in feed_own])
    contraction_grad = jnp.stack([share[:, hidden:].T for share in feed_own])
    return (
        stream.reshape(rows, block, width),
        upstream.reshape(rows, block, width),
        projection_grad,
        head_grad,
        mixing_grad,
        expansion_grad,
        hidden_grad,
        contraction_grad,
        gains_grad,
        offsets_grad,
    )


def solution(mesh):
    in_specs = (
        P("shard", "context", None),
        P("shard", "context"),
        P(None, None, "shard", "tensor"),
        P(None, None, "tensor", "shard"),
        P(None, "tensor", "shard"),
        P(None, "shard", "tensor"),
        P(None, "tensor", "shard"),
        P(None, "tensor", "shard"),
        P(None, None, "shard"),
        P(None, None, "shard"),
        P("shard", "context", None),
    )
    out_specs = (
        P("shard", "context", None),
        P("shard", "context", None),
        P(None, None, "shard", "tensor"),
        P(None, None, "tensor", "shard"),
        P(None, "tensor", "shard"),
        P(None, "shard", "tensor"),
        P(None, "tensor", "shard"),
        P(None, "tensor", "shard"),
        P(None, None, "shard"),
        P(None, None, "shard"),
    )
    return jax.shard_map(
        per_device, mesh=mesh, in_specs=in_specs, out_specs=out_specs, check_vma=False
    )
```

profile of v0, /device:TPU:0, one launch (start us, length us, event | category | flops | bytes accessed | tf_op | source)
XLA Modules:
  0.0 616.7 jit_solution(8124101954752828164)
XLA Ops:
  14.1 5.2 collective-permute-start.2
  19.3 2.6 collective-permute-start.3
  23.3 7.9 %all-to-all-start = ((bf16[16,8,128]{2,1,0:T(8,128)(2,1)}), bf16[16,8,128]{2,1,0:T(8,128)(2,1)S(1)}, u32[]{:S(2)}, u32[]{:S(2)}) async-start(bf16[16,8,128]{2,1,0:T(8,128)(2,1)} %broadcast_in_dim.34), calls=%async_computation | async-start | bytes 65536 | tf_op jit(solution)/shard_map/all_to_all | solution.py:127
  31.7 7.1 %all-to-all-done = bf16[16,8,128]{2,1,0:T(8,128)(2,1)S(1)} async-done(((bf16[16,8,128]{2,1,0:T(8,128)(2,1)}), bf16[16,8,128]{2,1,0:T(8,128)(2,1)S(1)}, u32[]{:S(2)}, u32[]{:S(2)}) %all-to-all-start) | async-done | bytes 32800 | tf_op jit(solution)/shard_map/all_to_all | solution.py:127
  42.3 39.0 %all-gather.3.cloned.1.call-done = bf16[768,4608]{1,0:T(8,128)(2,1)} async-done(((bf16[48,4608]{1,0:T(8,128)(2,1)}), bf16[768,4608]{1,0:T(8,128)(2,1)}) %all-gather.3.cloned.1.call-update) | async-done | bytes 7077904 | tf_op jit(solution)/shard_map/all_gather | solution.py:117
  83.5 4.9 collective-permute-start
  88.4 2.5 collective-permute-start.1
  91.4 6.5 %collective-permute-done = bf16[2,128,768]{2,1,0:T(8,128)(2,1)S(1)} collective-permute-done((bf16[2,128,768]{2,1,0:T(8,128)(2,1)S(1)}, bf16[2,128,768]{2,1,0:T(8,128)(2,1)S(1)}, u32[]{:S(2)}, u32[]{:S(2)}) %collective-permute-start) | collective-permute-done | bytes 393248 | tf_op jit(solution)/shard_map/ppermute | solution.py:55
  97.9 7.3 %collective-permute-done.1 = bf16[2,128,768]{2,1,0:T(8,128)(2,1)S(1)} collective-permute-done((bf16[2,128,768]{2,1,0:T(8,128)(2,1)S(1)}, bf16[2,128,768]{2,1,0:T(8,128)(2,1)S(1)}, u32[]{:S(2)}, u32[]{:S(2)}) %collective-permute-start.1) | collective-permute-done | bytes 393248 | tf_op jit(solution)/shard_map/ppermute | solution.py:55
  126.0 2.6 convolution_add_fusion.3
  128.6 4.2 fusion.15
  138.5 10.1 %all-gather.5.cloned.1.call-done = bf16[768,4608]{1,0:T(8,128)(2,1)} async-done(((bf16[48,4608]{1,0:T(8,128)(2,1)}), bf16[768,4608]{1,0:T(8,128)(2,1)}) %all-gather.5.cloned.1.call-update) | async-done | bytes 7077904 | tf_op jit(solution)/shard_map/all_gather | solution.py:117
  151.9 5.7 collective-permute-start.6
  157.6 3.4 collective-permute-start.7
  162.8 3.9 collective-permute-done.6
  166.7 7.3 %collective-permute-done.7 = bf16[2,128,768]{2,1,0:T(8,128)(2,1)} collective-permute-done((bf16[2,128,768]{2,1,0:T(8,128)(2,1)}, bf16[2,128,768]{2,1,0:T(8,128)(2,1)}, u32[]{:S(2)}, u32[]{:S(2)}) %collective-permute-start.7) | collective-permute-done | bytes 393248 | tf_op jit(solution)/shard_map/ppermute | solution.py:55
  184.6 2.6 fusion.49
  200.9 2.7 convolution_add_fusion.2
  203.6 4.2 fusion.135
  212.3 2.5 multiply_reduce_fusion
  214.8 3.5 fusion.119
  223.5 3.5 fusion.80
  228.9 2.7 copy.186
  231.6 2.6 fusion.100
  234.2 2.7 copy.185
  246.2 7.9 %collective-permute-done.11 = bf16[2,128,768]{2,1,0:T(8,128)(2,1)} collective-permute-done((bf16[2,128,768]{2,1,0:T(8,128)(2,1)}, bf16[2,128,768]{2,1,0:T(8,128)(2,1)}, u32[]{:S(2)}, u32[]{:S(2)}) %collective-permute-start.11) | collective-permute-done | bytes 393248 | tf_op jit(solution)/shard_map/ppermute | solution.py:60
  254.1 3.1 collective-permute-done.12
  272.3 2.5 multiply_reduce_fusion.2
  282.7 2.7 copy.195
  298.5 15.0 %collective-permute-done.15 = bf16[2,128,768]{2,1,0:T(8,128)(2,1)} collective-permute-done((bf16[2,128,768]{2,1,0:T(8,128)(2,1)}, bf16[2,128,768]{2,1,0:T(8,128)(2,1)}, u32[]{:S(2)}, u32[]{:S(2)}) %collective-permute-start.15) | collective-permute-done | bytes 393248 | tf_op jit(solution)/shard_map/ppermute | solution.py:60
  313.5 3.2 collective-permute-done.16
  325.4 2.7 pad_maximum_fusion.1
  332.5 2.7 pad_maximum_fusion
  352.5 5.3 all-to-all-start.1
  357.8 7.6 %all-to-all-done.1 = f32[16,8,128]{2,1,0:T(8,128)S(1)} async-done(((f32[16,8,128]{2,1,0:T(8,128)}), f32[16,8,128]{2,1,0:T(8,128)S(1)}, u32[]{:S(2)}, u32[]{:S(2)}) %all-to-all-start.1) | async-done | bytes 65568 | tf_op jit(solution)/shard_map/all_to_all | solution.py:313
  365.5 7.0 %collective-permute-start.24 = (f32[8,128]{1,0:T(8,128)S(1)}, f32[8,128]{1,0:T(8,128)S(1)}, u32[]{:S(2)}, u32[]{:S(2)}) collective-permute-start(f32[8,128]{1,0:T(8,128)S(1)} %reduce_sum.395), channel_id=1, source_target_pairs={{0,2},{2,4},{4,6},{6,0},{1,3},{3,5},{5,7},{7,1},{8,10},{10,12},{12... | collective-permute-start | bytes 12296 | tf_op jit(solution)/shard_map/ppermute | solution.py:67
  372.5 2.8 collective-permute-start.26
  377.8 3.8 collective-permute-start.22
  388.0 41.1 %reduce-scatter.5.cloned.1.call-done = bf16[48,1536]{1,0:T(8,128)(2,1)} async-done(((bf16[768,1536]{1,0:T(8,128)(2,1)}), bf16[48,1536]{1,0:T(8,128)(2,1)}) %reduce-scatter.5.cloned.1.call-update) | async-done | bytes 147472 | tf_op jit(solution)/shard_map/reduce_scatter | solution.py:212
  430.6 2.7 collective-permute-start.19
  439.6 70.3 %reduce-scatter.11.cloned.1.call-done = bf16[48,3072]{1,0:T(8,128)(2,1)} async-done(((bf16[768,3072]{1,0:T(8,128)(2,1)}), bf16[48,3072]{1,0:T(8,128)(2,1)}) %reduce-scatter.11.cloned.1.call-update) | async-done | bytes 294928 | tf_op jit(solution)/shard_map/reduce_scatter | solution.py:212
  511.4 2.7 collective-permute-start.31
  517.1 3.2 collective-permute-done.30
  520.3 5.5 collective-permute-done.31
  526.0 64.9 %reduce-scatter.9.cloned.1.call-done = bf16[48,3072]{1,0:T(8,128)(2,1)} async-done(((bf16[768,3072]{1,0:T(8,128)(2,1)}), bf16[48,3072]{1,0:T(8,128)(2,1)}) %reduce-scatter.9.cloned.1.call-update) | async-done | bytes 294928 | tf_op jit(solution)/shard_map/reduce_scatter | solution.py:212
  592.3 2.7 collective-permute-start.28
  596.5 4.8 collective-permute-done.27
  601.3 5.5 collective-permute-done.28
  (514 shorter events, 183.7 us)
Async XLA Ops:
  7.2 24.0 %copy-start.2 = (f32[2,128,768]{2,1,0:T(8,128)S(1)}, f32[2,128,768]{2,1,0:T(8,128)}, u32[]{:S(2)}) copy-start(f32[2,128,768]{2,1,0:T(8,128)} %param.11) | copy-start | bytes 2359300
  7.2 74.0 %all-gather.3.cloned.1.call-start = ((), (), s32[]{:S(2)}) async-start(), calls=%async_computation.6 | async-start | bytes 7520256 | tf_op jit(solution)/shard_map/all_gather | solution.py:117
  13.4 135.2 %all-gather.5.cloned.1.call-start = ((), (), s32[]{:S(2)}) async-start(), calls=%async_computation.7 | async-start | bytes 7520256 | tf_op jit(solution)/shard_map/all_gather | solution.py:117
  14.1 76.8 %collective-permute-start.2 = (s32[2,128]{1,0:T(2,128)S(1)}, s32[2,128]{1,0:T(2,128)S(1)}, u32[]{:S(2)}, u32[]{:S(2)}) collective-permute-start(s32[2,128]{1,0:T(2,128)S(1)} %copy-done.105), channel_id=1, source_target_pairs={{0,4},{2,6},{1,5},{3,7},{8,12},{10,14},{9,13},{11,15},{16,20},{18,... | collective-permute-start | bytes 3080 | tf_op jit(solution)/shard_map/ppermute | solution.py:55
  19.3 71.7 %collective-permute-start.3 = (s32[2,128]{1,0:T(2,128)S(1)}, s32[2,128]{1,0:T(2,128)S(1)}, u32[]{:S(2)}, u32[]{:S(2)}) collective-permute-start(s32[2,128]{1,0:T(2,128)S(1)} %copy-done.105), channel_id=1, source_target_pairs={{0,2},{2,4},{4,6},{1,3},{3,5},{5,7},{8,10},{10,12},{12,14},{9,11},... | collective-permute-start | bytes 3080 | tf_op jit(solution)/shard_map/ppermute | solution.py:55
  23.3 15.6 %all-to-all-start = ((bf16[16,8,128]{2,1,0:T(8,128)(2,1)}), bf16[16,8,128]{2,1,0:T(8,128)(2,1)S(1)}, u32[]{:S(2)}, u32[]{:S(2)}) async-start(bf16[16,8,128]{2,1,0:T(8,128)(2,1)} %broadcast_in_dim.34), calls=%async_computation | async-start | bytes 65536 | tf_op jit(solution)/shard_map/all_to_all | solution.py:127
  31.2 346.6 %reduce-scatter.7.cloned.1.call-start = ((), (), s32[]{:S(2)}) async-start(), calls=%async_computation.9 | async-start | bytes 2506752 | tf_op jit(solution)/shard_map/reduce_scatter | solution.py:212
  31.4 52.0 %copy-start.80 = (f32[256]{0:T(256)}, f32[256]{0:T(256)S(1)}, u32[]{:S(2)}) copy-start(f32[256]{0:T(256)S(1)} %get-tuple-element.151) | copy-start | bytes 3076
  31.7 51.7 %copy-start.82 = (f32[256]{0:T(256)}, f32[256]{0:T(256)S(1)}, u32[]{:S(2)}) copy-start(f32[256]{0:T(256)S(1)} %rsqrt_bitcast_fusion) | copy-start | bytes 3076
  40.8 42.6 %copy-start.58 = (f32[768]{0:T(1024)}, f32[768]{0:T(1024)S(1)}, u32[]{:S(2)}) copy-start(f32[768]{0:T(1024)S(1)} %mul.315) | copy-start | bytes 9220
  42.3 39.0 %copy-start.42 = (bf16[256,768]{1,0:T(8,128)(2,1)}, bf16[256,768]{1,0:T(8,128)(2,1)S(1)}, u32[]{:S(2)}) copy-start(bf16[256,768]{1,0:T(8,128)(2,1)S(1)} %add_convert_fusion.3) | copy-start | bytes 1179652
  83.5 14.5 %collective-permute-start = (bf16[2,128,768]{2,1,0:T(8,128)(2,1)S(1)}, bf16[2,128,768]{2,1,0:T(8,128)(2,1)S(1)}, u32[]{:S(2)}, u32[]{:S(2)}) collective-permute-start(bf16[2,128,768]{2,1,0:T(8,128)(2,1)S(1)} %bitcast.247), channel_id=1, source_target_pairs={{0,4},{2,6},{1,5},{3,7},{8,12},{10,14},{9,13},{11,15},{16,20},{18,... | collective-permute-start | bytes 1179656 | tf_op jit(solution)/shard_map/ppermute | solution.py:55
  88.4 16.8 %collective-permute-start.1 = (bf16[2,128,768]{2,1,0:T(8,128)(2,1)S(1)}, bf16[2,128,768]{2,1,0:T(8,128)(2,1)S(1)}, u32[]{:S(2)}, u32[]{:S(2)}) collective-permute-start(bf16[2,128,768]{2,1,0:T(8,128)(2,1)S(1)} %bitcast.248), channel_id=1, source_target_pairs={{0,2},{2,4},{4,6},{1,3},{3,5},{5,7},{8,10},{10,12},{12,14},{9,11},... | collective-permute-start | bytes 1179656 | tf_op jit(solution)/shard_map/ppermute | solution.py:55
  114.4 8.5 %collective-permute-start.4 = (f32[256,768]{1,0:T(8,128)}, f32[256,768]{1,0:T(8,128)}, u32[]{:S(2)}, u32[]{:S(2)}) collective-permute-start(f32[256,768]{1,0:T(8,128)} %fusion.74), channel_id=1, source_target_pairs={{0,1},{1,0},{2,3},{3,2},{4,5},{5,4},{6,7},{7,6},{8,9},{9,8},{10,11... | collective-permute-start | bytes 2359304 | tf_op jit(solution)/shard_map/ppermute | solution.py:49
  132.9 2.7 collective-permute-start.5
  151.9 14.8 %collective-permute-start.6 = (bf16[2,128,768]{2,1,0:T(8,128)(2,1)}, bf16[2,128,768]{2,1,0:T(8,128)(2,1)}, u32[]{:S(2)}, u32[]{:S(2)}) collective-permute-start(bf16[2,128,768]{2,1,0:T(8,128)(2,1)} %bitcast.30), channel_id=1, source_target_pairs={{0,4},{2,6},{1,5},{3,7},{8,12},{10,14},{9,13},{11,15},{16,20},{18,... | collective-permute-start | bytes 1179656 | tf_op jit(solution)/shard_map/ppermute | solution.py:55
  157.6 16.4 %collective-permute-start.7 = (bf16[2,128,768]{2,1,0:T(8,128)(2,1)}, bf16[2,128,768]{2,1,0:T(8,128)(2,1)}, u32[]{:S(2)}, u32[]{:S(2)}) collective-permute-start(bf16[2,128,768]{2,1,0:T(8,128)(2,1)} %bitcast.30), channel_id=1, source_target_pairs={{0,2},{2,4},{4,6},{1,3},{3,5},{5,7},{8,10},{10,12},{12,14},{9,11},... | collective-permute-start | bytes 1179656 | tf_op jit(solution)/shard_map/ppermute | solution.py:55
  189.9 8.8 %collective-permute-start.8 = (f32[256,768]{1,0:T(8,128)}, f32[256,768]{1,0:T(8,128)}, u32[]{:S(2)}, u32[]{:S(2)}) collective-permute-start(f32[256,768]{1,0:T(8,128)} %fusion.71), channel_id=1, source_target_pairs={{0,1},{1,0},{2,3},{3,2},{4,5},{5,4},{6,7},{7,6},{8,9},{9,8},{10,11... | collective-permute-start | bytes 2359304 | tf_op jit(solution)/shard_map/ppermute | solution.py:49
  209.5 2.8 collective-permute-start.10
  212.0 2.8 collective-permute-start.9
  239.6 14.4 %collective-permute-start.11 = (bf16[2,128,768]{2,1,0:T(8,128)(2,1)}, bf16[2,128,768]{2,1,0:T(8,128)(2,1)}, u32[]{:S(2)}, u32[]{:S(2)}) collective-permute-start(bf16[2,128,768]{2,1,0:T(8,128)(2,1)} %get-tuple-element.106), channel_id=1, source_target_pairs={{2,0},{4,2},{6,4},{3,1},{5,3},{7,5},{10,8},{12,10},{14,12},{11,9},... | collective-permute-start | bytes 1179656 | tf_op jit(solution)/shard_map/ppermute | solution.py:60
  240.9 16.2 %collective-permute-start.12 = (bf16[2,128,768]{2,1,0:T(8,128)(2,1)}, bf16[2,128,768]{2,1,0:T(8,128)(2,1)}, u32[]{:S(2)}, u32[]{:S(2)}) collective-permute-start(bf16[2,128,768]{2,1,0:T(8,128)(2,1)} %get-tuple-element.107), channel_id=1, source_target_pairs={{4,0},{6,2},{5,1},{7,3},{12,8},{14,10},{13,9},{15,11},{20,16},{22,... | collective-permute-start | bytes 1179656 | tf_op jit(solution)/shard_map/ppermute | solution.py:60
  262.1 2.0 collective-permute-start.13
  270.0 2.1 collective-permute-start.14
  271.7 157.4 %reduce-scatter.5.cloned.1.call-start = ((), (), s32[]{:S(2)}) async-start(), calls=%async_computation.8 | async-start | bytes 2506752 | tf_op jit(solution)/shard_map/reduce_scatter | solution.py:212
  293.6 20.0 %collective-permute-start.15 = (bf16[2,128,768]{2,1,0:T(8,128)(2,1)}, bf16[2,128,768]{2,1,0:T(8,128)(2,1)}, u32[]{:S(2)}, u32[]{:S(2)}) collective-permute-start(bf16[2,128,768]{2,1,0:T(8,128)(2,1)} %get-tuple-element.104), channel_id=1, source_target_pairs={{2,0},{4,2},{6,4},{3,1},{5,3},{7,5},{10,8},{12,10},{14,12},{11,9},... | collective-permute-start | bytes 1179656 | tf_op jit(solution)/shard_map/ppermute | solution.py:60
  294.9 21.9 %collective-permute-start.16 = (bf16[2,128,768]{2,1,0:T(8,128)(2,1)}, bf16[2,128,768]{2,1,0:T(8,128)(2,1)}, u32[]{:S(2)}, u32[]{:S(2)}) collective-permute-start(bf16[2,128,768]{2,1,0:T(8,128)(2,1)} %get-tuple-element.105), channel_id=1, source_target_pairs={{4,0},{6,2},{5,1},{7,3},{12,8},{14,10},{13,9},{15,11},{20,16},{22,... | collective-permute-start | bytes 1179656 | tf_op jit(solution)/shard_map/ppermute | solution.py:60
  298.1 20.8 %copy-start.48 = (bf16[256,384]{1,0:T(8,128)(2,1)}, bf16[256,384]{1,0:T(8,128)(2,1)S(1)}, u32[]{:S(2)}) copy-start(bf16[256,384]{1,0:T(8,128)(2,1)S(1)} %copy.196) | copy-start | bytes 589828
  321.3 188.7 %reduce-scatter.11.cloned.1.call-start = ((), (), s32[]{:S(2)}) async-start(), calls=%async_computation.11 | async-start | bytes 5013504 | tf_op jit(solution)/shard_map/reduce_scatter | solution.py:212
  328.2 262.7 %reduce-scatter.9.cloned.1.call-start = ((), (), s32[]{:S(2)}) async-start(), calls=%async_computation.10 | async-start | bytes 5013504 | tf_op jit(solution)/shard_map/reduce_scatter | solution.py:212
  343.3 6.8 %collective-permute-start.17 = (bf16[256,768]{1,0:T(8,128)(2,1)S(1)}, bf16[256,768]{1,0:T(8,128)(2,1)S(1)}, u32[]{:S(2)}, u32[]{:S(2)}) collective-permute-start(bf16[256,768]{1,0:T(8,128)(2,1)S(1)} %fusion.36), channel_id=1, source_target_pairs={{0,1},{1,0},{2,3},{3,2},{4,5},{5,4},{6,7},{7,6},{8,9},{9,8},{10,11... | collective-permute-start | bytes 1179656 | tf_op jit(solution)/shard_map/ppermute | solution.py:49
  349.0 26.3 %copy-start.83 = (f32[256]{0:T(256)S(1)}, f32[256]{0:T(256)}, u32[]{:S(2)}) copy-start(f32[256]{0:T(256)} %copy-done.82) | copy-start | bytes 3076
  352.5 12.9 %all-to-all-start.1 = ((f32[16,8,128]{2,1,0:T(8,128)}), f32[16,8,128]{2,1,0:T(8,128)S(1)}, u32[]{:S(2)}, u32[]{:S(2)}) async-start(f32[16,8,128]{2,1,0:T(8,128)} %bitcast.123), calls=%async_computation.3 | async-start | bytes 131072 | tf_op jit(solution)/shard_map/all_to_all | solution.py:313
  365.5 11.0 %collective-permute-start.24 = (f32[8,128]{1,0:T(8,128)S(1)}, f32[8,128]{1,0:T(8,128)S(1)}, u32[]{:S(2)}, u32[]{:S(2)}) collective-permute-start(f32[8,128]{1,0:T(8,128)S(1)} %reduce_sum.395), channel_id=1, source_target_pairs={{0,2},{2,4},{4,6},{6,0},{1,3},{3,5},{5,7},{7,1},{8,10},{10,12},{12... | collective-permute-start | bytes 12296 | tf_op jit(solution)/shard_map/ppermute | solution.py:67
  372.5 5.1 collective-permute-start.25
  372.5 5.1 collective-permute-start.26
  377.7 7.7 %collective-permute-start.21 = (bf16[48,1536]{1,0:T(8,128)(2,1)}, bf16[48,1536]{1,0:T(8,128)(2,1)S(1)}, u32[]{:S(2)}, u32[]{:S(2)}) collective-permute-start(bf16[48,1536]{1,0:T(8,128)(2,1)} %reduce-scatter.7.cloned.1.call-done), channel_id=1, source_target_pairs={{0,2},{2,4},{4,6},{6,0},{1,3},{3,5},{5,7},{7,1},{8,10},{10,12},{12... | collective-permute-start | bytes 442376 | tf_op jit(solution)/shard_map/ppermute | solution.py:67
  377.8 8.8 %collective-permute-start.22 = (bf16[48,1536]{1,0:T(8,128)(2,1)}, bf16[48,1536]{1,0:T(8,128)(2,1)S(1)}, u32[]{:S(2)}, u32[]{:S(2)}) collective-permute-start(bf16[48,1536]{1,0:T(8,128)(2,1)} %reduce-scatter.7.cloned.1.call-done), channel_id=1, source_target_pairs={{0,4},{2,6},{4,0},{6,2},{1,5},{3,7},{5,1},{7,3},{8,12},{10,14},{12... | collective-permute-start | bytes 442376 | tf_op jit(solution)/shard_map/ppermute | solution.py:67
  381.7 5.4 collective-permute-start.23
  429.1 7.9 %collective-permute-start.18 = (bf16[48,1536]{1,0:T(8,128)(2,1)}, bf16[48,1536]{1,0:T(8,128)(2,1)S(1)}, u32[]{:S(2)}, u32[]{:S(2)}) collective-permute-start(bf16[48,1536]{1,0:T(8,128)(2,1)} %reduce-scatter.5.cloned.1.call-done), channel_id=1, source_target_pairs={{0,2},{2,4},{4,6},{6,0},{1,3},{3,5},{5,7},{7,1},{8,10},{10,12},{12... | collective-permute-start | bytes 442376 | tf_op jit(solution)/shard_map/ppermute | solution.py:67
  430.6 8.0 %collective-permute-start.19 = (bf16[48,1536]{1,0:T(8,128)(2,1)}, bf16[48,1536]{1,0:T(8,128)(2,1)S(1)}, u32[]{:S(2)}, u32[]{:S(2)}) collective-permute-start(bf16[48,1536]{1,0:T(8,128)(2,1)} %reduce-scatter.5.cloned.1.call-done), channel_id=1, source_target_pairs={{0,4},{2,6},{4,0},{6,2},{1,5},{3,7},{5,1},{7,3},{8,12},{10,14},{12... | collective-permute-start | bytes 442376 | tf_op jit(solution)/shard_map/ppermute | solution.py:67
  433.3 5.4 collective-permute-start.20
  509.9 10.4 %collective-permute-start.30 = (bf16[48,3072]{1,0:T(8,128)(2,1)}, bf16[48,3072]{1,0:T(8,128)(2,1)S(1)}, u32[]{:S(2)}, u32[]{:S(2)}) collective-permute-start(bf16[48,3072]{1,0:T(8,128)(2,1)} %reduce-scatter.11.cloned.1.call-done), channel_id=1, source_target_pairs={{0,2},{2,4},{4,6},{6,0},{1,3},{3,5},{5,7},{7,1},{8,10},{10,12},{12... | collective-permute-start | bytes 884744 | tf_op jit(solution)/shard_map/ppermute | solution.py:67
  511.4 14.4 %collective-permute-start.31 = (bf16[48,3072]{1,0:T(8,128)(2,1)}, bf16[48,3072]{1,0:T(8,128)(2,1)S(1)}, u32[]{:S(2)}, u32[]{:S(2)}) collective-permute-start(bf16[48,3072]{1,0:T(8,128)(2,1)} %reduce-scatter.11.cloned.1.call-done), channel_id=1, source_target_pairs={{0,4},{2,6},{4,0},{6,2},{1,5},{3,7},{5,1},{7,3},{8,12},{10,14},{12... | collective-permute-start | bytes 884744 | tf_op jit(solution)/shard_map/ppermute | solution.py:67
  514.1 11.7 %collective-permute-start.32 = (bf16[48,3072]{1,0:T(8,128)(2,1)}, bf16[48,3072]{1,0:T(8,128)(2,1)S(1)}, u32[]{:S(2)}, u32[]{:S(2)}) collective-permute-start(bf16[48,3072]{1,0:T(8,128)(2,1)} %reduce-scatter.11.cloned.1.call-done), channel_id=1, source_target_pairs={{0,6},{2,0},{4,2},{6,4},{1,7},{3,1},{5,3},{7,5},{8,14},{10,8},{12,... | collective-permute-start | bytes 884744 | tf_op jit(solution)/shard_map/ppermute | solution.py:67
  590.9 10.4 %collective-permute-start.27 = (bf16[48,3072]{1,0:T(8,128)(2,1)}, bf16[48,3072]{1,0:T(8,128)(2,1)S(1)}, u32[]{:S(2)}, u32[]{:S(2)}) collective-permute-start(bf16[48,3072]{1,0:T(8,128)(2,1)} %reduce-scatter.9.cloned.1.call-done), channel_id=1, source_target_pairs={{0,2},{2,4},{4,6},{6,0},{1,3},{3,5},{5,7},{7,1},{8,10},{10,12},{12... | collective-permute-start | bytes 884744 | tf_op jit(solution)/shard_map/ppermute | solution.py:67
  592.3 14.4 %collective-permute-start.28 = (bf16[48,3072]{1,0:T(8,128)(2,1)}, bf16[48,3072]{1,0:T(8,128)(2,1)S(1)}, u32[]{:S(2)}, u32[]{:S(2)}) collective-permute-start(bf16[48,3072]{1,0:T(8,128)(2,1)} %reduce-scatter.9.cloned.1.call-done), channel_id=1, source_target_pairs={{0,4},{2,6},{4,0},{6,2},{1,5},{3,7},{5,1},{7,3},{8,12},{10,14},{12... | collective-permute-start | bytes 884744 | tf_op jit(solution)/shard_map/ppermute | solution.py:67
  595.0 11.7 %collective-permute-start.29 = (bf16[48,3072]{1,0:T(8,128)(2,1)}, bf16[48,3072]{1,0:T(8,128)(2,1)S(1)}, u32[]{:S(2)}, u32[]{:S(2)}) collective-permute-start(bf16[48,3072]{1,0:T(8,128)(2,1)} %reduce-scatter.9.cloned.1.call-done), channel_id=1, source_target_pairs={{0,6},{2,0},{4,2},{6,4},{1,7},{3,1},{5,3},{7,5},{8,14},{10,8},{12,... | collective-permute-start | bytes 884744 | tf_op jit(solution)/shard_map/ppermute | solution.py:67
  (112 other events, 574.6 us)
Sparse Core Ops, SparseCore 0:
  13.5 67.7 all-gather.2
  83.9 64.6 all-gather.4
  271.8 79.7 reduce-scatter.6
  354.8 74.2 reduce-scatter.4
  432.3 77.6 reduce-scatter.10
  513.1 77.6 reduce-scatter.8
where the time goes:
time: 627 us; the launch traced here: 617 us
  waiting for transfers between devices  323 us (52%)
  local copies, waits for them, and re-layouts  82.9 us (13%)
  starting transfers between devices  76.2 us (12%)
  matrix products  68.4 us (11%)
  other arithmetic  50.4 us (8%)
  between operations  16.2 us (3%)
    reduce_scatter x4, waiting for transfers between devices, scatter(): return lax.psum_scatter(packed, 'shard', scatter_dimension=0, tiled=True)  176 us
    all_gather x2, waiting for transfers between devices, per_device(): gathered.append(lax.all_gather(packed, 'shard', axis=0, tiled=True))  49.1 us
    dot_general x24, matrix products, dot(): lax.dot_general(left, right, (((left_dim,), (right_dim,)), ((), ())), pre...  46.1 us
    ppermute x15, starting transfers between devices, context_sum(): lax.ppermute(part, 'context', [(i, (i + steps) % size) for i in range(siz...  31.3 us
    ppermute x4, waiting for transfers between devices, from_after(): lax.ppermute(block, 'context', [(i + steps, i) for i in range(size - step...  29.2 us
    ppermute x15, waiting for transfers between devices, context_sum(): lax.ppermute(part, 'context', [(i, (i + steps) % size) for i in range(siz...  25.6 us
    ppermute x6, waiting for transfers between devices, from_before(): lax.ppermute(block, 'context', [(i, i + steps) for i in range(size - step...  25 us
    ppermute x6, starting transfers between devices, from_before(): lax.ppermute(block, 'context', [(i, i + steps) for i in range(size - step...  24.3 us
  transfers between devices with their start and end apart: 41, of which 26 were waited for; matrix products, arithmetic and copies ran while one was open for 19% of the time, Pallas kernels for 0%

commit v1 on v0

--- a/solution.py
+++ b/solution.py
@@ -114,7 +114,11 @@
             ],
             axis=1,
         )
-        gathered.append(lax.all_gather(packed, "shard", axis=0, tiled=True))
+        gathered.append(
+            jnp.concatenate(
+                lax.all_to_all(jnp.stack([packed] * lax.axis_size("shard")), "shard", 0, 0), axis=0
+            )
+        )
     small_parts = [norm_gains, offsets, head_bias, hidden_bias]
     small_sizes = [part.size for part in small_parts]
     small_total = sum(small_sizes)

time: 627 us -> 733 us (1.17)
  waiting for transfers between devices: 323 us -> 402 us
  starting transfers between devices: 76.2 us -> 86.9 us
  local copies, waits for them, and re-layouts: 82.9 us -> 91.9 us
    all_to_all x0 -> x2, waiting for transfers between devices: none -> 138 us  [per_device(): lax.all_to_all(jnp.stack([packed] * lax.axis_size('shard')), 'shard', 0, 0)]
    all_gather x2 -> x0, waiting for transfers between devices: 49.1 us -> none  [per_device(): gathered.append(lax.all_gather(packed, 'shard', axis=0, tiled=True))]
    all_to_all x0 -> x2, starting transfers between devices: none -> 10.4 us  [per_device(): lax.all_to_all(jnp.stack([packed] * lax.axis_size('shard')), 'shard', 0, 0)]
    unnamed x253 -> x233, local copies, waits for them, and re-layouts: 22.8 us -> 23.3 us
  transfers between devices with their start and end apart: 41 -> 41, of which waited for: 26 -> 26; matrix products, arithmetic and copies ran while one was open for 19% -> 18% of each run, Pallas kernels for 0% -> 0%
where the time goes in v1:
time: 733 us; the launch traced here: 722 us
  waiting for transfers between devices  402 us (55%)
  local copies, waits for them, and re-layouts  91.9 us (13%)
  starting transfers between devices  86.9 us (12%)
  matrix products  75.4 us (10%)
  other arithmetic  50.2 us (7%)
  between operations  15.7 us (2%)
    reduce_scatter x4, waiting for transfers between devices, scatter(): return lax.psum_scatter(packed, 'shard', scatter_dimension=0, tiled=True)  177 us
    all_to_all x2, waiting for transfers between devices, per_device(): lax.all_to_all(jnp.stack([packed] * lax.axis_size('shard')), 'shard', 0, 0)  138 us
    dot_general x24, matrix products, dot(): lax.dot_general(left, right, (((left_dim,), (right_dim,)), ((), ())), pre...  53.1 us
    ppermute x15, starting transfers between devices, context_sum(): lax.ppermute(part, 'context', [(i, (i + steps) % size) for i in range(siz...  31.2 us
    ppermute x4, waiting for transfers between devices, from_after(): lax.ppermute(block, 'context', [(i + steps, i) for i in range(size - step...  29.1 us
    ppermute x15, waiting for transfers between devices, context_sum(): lax.ppermute(part, 'context', [(i, (i + steps) % size) for i in range(siz...  25.5 us
    ppermute x6, starting transfers between devices, from_before(): lax.ppermute(block, 'context', [(i, i + steps) for i in range(size - step...  24.6 us
    unnamed x233, local copies, waits for them, and re-layouts  23.3 us
  transfers between devices with their start and end apart: 41, of which 26 were waited for; matrix products, arithmetic and copies ran while one was open for 18% of the time, Pallas kernels for 0%

profile of v1, /device:TPU:0, one launch (start us, length us, event | category | flops | bytes accessed | tf_op | source)
XLA Modules:
  0.0 721.6 jit_solution(13641795393796039970)
XLA Ops:
  11.2 8.0 %all-to-all-start = ((bf16[16,8,128]{2,1,0:T(8,128)(2,1)}), bf16[16,8,128]{2,1,0:T(8,128)(2,1)S(1)}, u32[]{:S(2)}, u32[]{:S(2)}) async-start(bf16[16,8,128]{2,1,0:T(8,128)(2,1)} %broadcast_in_dim.34), calls=%async_computation | async-start | bytes 65536 | tf_op jit(solution)/shard_map/all_to_all | solution.py:131
  26.8 3.6 stack.174
  30.4 5.0 all-to-all-start.1
  35.5 5.1 collective-permute-start.2
  46.5 92.8 %all-to-all-done.1 = bf16[16,48,4608]{2,1,0:T(8,128)(2,1)} async-done(((bf16[16,48,4608]{2,1,0:T(8,128)(2,1)}), bf16[16,48,4608]{2,1,0:T(8,128)(2,1)}, u32[]{:S(2)}, u32[]{:S(2)}) %all-to-all-start.1) | async-done | bytes 7077920 | tf_op jit(solution)/shard_map/all_to_all | solution.py:119
  139.3 3.5 stack.175
  142.8 5.4 all-to-all-start.2
  151.0 5.1 collective-permute-start
  159.2 6.5 collective-permute-done
  165.7 5.3 collective-permute-done.1
  194.2 4.2 fusion.15
  204.3 45.3 %all-to-all-done.2 = bf16[16,48,4608]{2,1,0:T(8,128)(2,1)} async-done(((bf16[16,48,4608]{2,1,0:T(8,128)(2,1)}), bf16[16,48,4608]{2,1,0:T(8,128)(2,1)}, u32[]{:S(2)}, u32[]{:S(2)}) %all-to-all-start.2) | async-done | bytes 7077920 | tf_op jit(solution)/shard_map/all_to_all | solution.py:119
  252.9 5.9 collective-permute-start.6
  258.8 3.3 collective-permute-start.7
  263.9 3.9 collective-permute-done.6
  267.9 4.4 collective-permute-done.7
  301.8 4.2 fusion.135
  306.0 3.5 fusion.45
  310.0 3.6 fusion.9
  316.5 3.5 fusion.119
  325.2 3.5 fusion.80
  330.6 2.7 copy.186
  333.3 2.7 fusion.100
  335.9 2.7 copy.185
  348.0 7.9 %collective-permute-done.11 = bf16[2,128,768]{2,1,0:T(8,128)(2,1)} collective-permute-done((bf16[2,128,768]{2,1,0:T(8,128)(2,1)}, bf16[2,128,768]{2,1,0:T(8,128)(2,1)}, u32[]{:S(2)}, u32[]{:S(2)}) %collective-permute-start.11) | collective-permute-done | bytes 393248 | tf_op jit(solution)/shard_map/ppermute | solution.py:60
  355.9 3.1 collective-permute-done.12
  368.1 3.6 fusion.136
  371.7 3.5 fusion.42
  388.0 2.7 copy.195
  403.7 15.0 %collective-permute-done.15 = bf16[2,128,768]{2,1,0:T(8,128)(2,1)} collective-permute-done((bf16[2,128,768]{2,1,0:T(8,128)(2,1)}, bf16[2,128,768]{2,1,0:T(8,128)(2,1)}, u32[]{:S(2)}, u32[]{:S(2)}) %collective-permute-start.15) | collective-permute-done | bytes 393248 | tf_op jit(solution)/shard_map/ppermute | solution.py:60
  418.7 3.2 collective-permute-done.16
  430.6 2.8 pad_maximum_fusion.1
  437.6 2.7 pad_maximum_fusion
  457.8 5.1 all-to-all-start.3
  462.9 7.6 %all-to-all-done.3 = f32[16,8,128]{2,1,0:T(8,128)S(1)} async-done(((f32[16,8,128]{2,1,0:T(8,128)}), f32[16,8,128]{2,1,0:T(8,128)S(1)}, u32[]{:S(2)}, u32[]{:S(2)}) %all-to-all-start.3) | async-done | bytes 65568 | tf_op jit(solution)/shard_map/all_to_all | solution.py:317
  470.6 7.1 collective-permute-start.24
  477.7 2.8 collective-permute-start.26
  483.0 3.8 collective-permute-start.22
  493.2 41.1 %reduce-scatter.5.cloned.1.call-done = bf16[48,1536]{1,0:T(8,128)(2,1)} async-done(((bf16[768,1536]{1,0:T(8,128)(2,1)}), bf16[48,1536]{1,0:T(8,128)(2,1)}) %reduce-scatter.5.cloned.1.call-update) | async-done | bytes 147472 | tf_op jit(solution)/shard_map/reduce_scatter | solution.py:216
  535.8 2.7 collective-permute-start.19
  544.8 70.4 %reduce-scatter.11.cloned.1.call-done = bf16[48,3072]{1,0:T(8,128)(2,1)} async-done(((bf16[768,3072]{1,0:T(8,128)(2,1)}), bf16[48,3072]{1,0:T(8,128)(2,1)}) %reduce-scatter.11.cloned.1.call-update) | async-done | bytes 294928 | tf_op jit(solution)/shard_map/reduce_scatter | solution.py:216
  616.6 2.8 collective-permute-start.31
  622.3 3.3 collective-permute-done.30
  625.7 5.4 collective-permute-done.31
  631.2 65.0 %reduce-scatter.9.cloned.1.call-done = bf16[48,3072]{1,0:T(8,128)(2,1)} async-done(((bf16[768,3072]{1,0:T(8,128)(2,1)}), bf16[48,3072]{1,0:T(8,128)(2,1)}) %reduce-scatter.9.cloned.1.call-update) | async-done | bytes 294928 | tf_op jit(solution)/shard_map/reduce_scatter | solution.py:216
  697.6 2.8 collective-permute-start.28
  701.8 4.8 collective-permute-done.27
  706.6 5.4 collective-permute-done.28
  (492 shorter events, 197.6 us)
Async XLA Ops:
  11.2 15.6 %all-to-all-start = ((bf16[16,8,128]{2,1,0:T(8,128)(2,1)}), bf16[16,8,128]{2,1,0:T(8,128)(2,1)S(1)}, u32[]{:S(2)}, u32[]{:S(2)}) async-start(bf16[16,8,128]{2,1,0:T(8,128)(2,1)} %broadcast_in_dim.34), calls=%async_computation | async-start | bytes 65536 | tf_op jit(solution)/shard_map/all_to_all | solution.py:131
  30.4 108.8 %all-to-all-start.1 = ((bf16[16,48,4608]{2,1,0:T(8,128)(2,1)}), bf16[16,48,4608]{2,1,0:T(8,128)(2,1)}, u32[]{:S(2)}, u32[]{:S(2)}) async-start(bf16[16,48,4608]{2,1,0:T(8,128)(2,1)} %stack.174), calls=%async_computation.1 | async-start | bytes 14155776 | tf_op jit(solution)/shard_map/all_to_all | solution.py:119
  35.5 123.3 %collective-permute-start.2 = (s32[2,128]{1,0:T(2,128)S(1)}, s32[2,128]{1,0:T(2,128)S(1)}, u32[]{:S(2)}, u32[]{:S(2)}) collective-permute-start(s32[2,128]{1,0:T(2,128)S(1)} %copy-done.103), channel_id=1, source_target_pairs={{0,4},{2,6},{1,5},{3,7},{8,12},{10,14},{9,13},{11,15},{16,20},{18,... | collective-permute-start | bytes 3080 | tf_op jit(solution)/shard_map/ppermute | solution.py:55
  40.6 118.2 %collective-permute-start.3 = (s32[2,128]{1,0:T(2,128)S(1)}, s32[2,128]{1,0:T(2,128)S(1)}, u32[]{:S(2)}, u32[]{:S(2)}) collective-permute-start(s32[2,128]{1,0:T(2,128)S(1)} %copy-done.103), channel_id=1, source_target_pairs={{0,2},{2,4},{4,6},{1,3},{3,5},{5,7},{8,10},{10,12},{12,14},{9,11},... | collective-permute-start | bytes 3080 | tf_op jit(solution)/shard_map/ppermute | solution.py:55
  43.3 99.4 %copy-start.78 = (f32[256]{0:T(256)}, f32[256]{0:T(256)S(1)}, u32[]{:S(2)}) copy-start(f32[256]{0:T(256)S(1)} %get-tuple-element.151) | copy-start | bytes 3076
  43.6 99.2 %copy-start.80 = (f32[256]{0:T(256)}, f32[256]{0:T(256)S(1)}, u32[]{:S(2)}) copy-start(f32[256]{0:T(256)S(1)} %rsqrt_bitcast_fusion) | copy-start | bytes 3076
  45.6 97.2 %copy-start.56 = (f32[768]{0:T(1024)}, f32[768]{0:T(1024)S(1)}, u32[]{:S(2)}) copy-start(f32[768]{0:T(1024)S(1)} %mul.315) | copy-start | bytes 9220
  46.5 102.4 %copy-start.42 = (bf16[256,768]{1,0:T(8,128)(2,1)}, bf16[256,768]{1,0:T(8,128)(2,1)S(1)}, u32[]{:S(2)}) copy-start(bf16[256,768]{1,0:T(8,128)(2,1)S(1)} %add_convert_fusion.3) | copy-start | bytes 1179652
  142.8 106.8 %all-to-all-start.2 = ((bf16[16,48,4608]{2,1,0:T(8,128)(2,1)}), bf16[16,48,4608]{2,1,0:T(8,128)(2,1)}, u32[]{:S(2)}, u32[]{:S(2)}) async-start(bf16[16,48,4608]{2,1,0:T(8,128)(2,1)} %stack.175), calls=%async_computation.2 | async-start | bytes 14155776 | tf_op jit(solution)/shard_map/all_to_all | solution.py:119
  148.2 334.8 %reduce-scatter.7.cloned.1.call-start = ((), (), s32[]{:S(2)}) async-start(), calls=%async_computation.9 | async-start | bytes 2506752 | tf_op jit(solution)/shard_map/reduce_scatter | solution.py:216
  151.0 14.7 %collective-permute-start = (bf16[2,128,768]{2,1,0:T(8,128)(2,1)S(1)}, bf16[2,128,768]{2,1,0:T(8,128)(2,1)S(1)}, u32[]{:S(2)}, u32[]{:S(2)}) collective-permute-start(bf16[2,128,768]{2,1,0:T(8,128)(2,1)S(1)} %bitcast.249), channel_id=1, source_target_pairs={{0,4},{2,6},{1,5},{3,7},{8,12},{10,14},{9,13},{11,15},{16,20},{18,... | collective-permute-start | bytes 1179656 | tf_op jit(solution)/shard_map/ppermute | solution.py:55
  156.2 14.8 %collective-permute-start.1 = (bf16[2,128,768]{2,1,0:T(8,128)(2,1)S(1)}, bf16[2,128,768]{2,1,0:T(8,128)(2,1)S(1)}, u32[]{:S(2)}, u32[]{:S(2)}) collective-permute-start(bf16[2,128,768]{2,1,0:T(8,128)(2,1)S(1)} %bitcast.250), channel_id=1, source_target_pairs={{0,2},{2,4},{4,6},{1,3},{3,5},{5,7},{8,10},{10,12},{12,14},{9,11},... | collective-permute-start | bytes 1179656 | tf_op jit(solution)/shard_map/ppermute | solution.py:55
  180.1 8.5 %collective-permute-start.4 = (f32[256,768]{1,0:T(8,128)}, f32[256,768]{1,0:T(8,128)}, u32[]{:S(2)}, u32[]{:S(2)}) collective-permute-start(f32[256,768]{1,0:T(8,128)} %fusion.74), channel_id=1, source_target_pairs={{0,1},{1,0},{2,3},{3,2},{4,5},{5,4},{6,7},{7,6},{8,9},{9,8},{10,11... | collective-permute-start | bytes 2359304 | tf_op jit(solution)/shard_map/ppermute | solution.py:49
  198.4 2.9 collective-permute-start.5
  199.3 50.3 %copy-start.60 = (f32[768]{0:T(1024)}, f32[768]{0:T(1024)S(1)}, u32[]{:S(2)}) copy-start(f32[768]{0:T(1024)S(1)} %mul.335) | copy-start | bytes 9220
  199.3 50.3 %copy-start.93 = (f32[768]{0:T(1024)}, f32[768]{0:T(1024)S(1)}, u32[]{:S(2)}) copy-start(f32[768]{0:T(1024)S(1)} %add.345) | copy-start | bytes 9220
  199.3 50.3 %copy-start.102 = (f32[1152]{0:T(1024)S(1)}, f32[1152]{0:T(1024)}, u32[]{:S(2)}) copy-start(f32[1152]{0:T(1024)} %get-tuple-element.149) | copy-start | bytes 13828
  252.9 15.0 %collective-permute-start.6 = (bf16[2,128,768]{2,1,0:T(8,128)(2,1)}, bf16[2,128,768]{2,1,0:T(8,128)(2,1)}, u32[]{:S(2)}, u32[]{:S(2)}) collective-permute-start(bf16[2,128,768]{2,1,0:T(8,128)(2,1)} %bitcast.32), channel_id=1, source_target_pairs={{0,4},{2,6},{1,5},{3,7},{8,12},{10,14},{9,13},{11,15},{16,20},{18,... | collective-permute-start | bytes 1179656 | tf_op jit(solution)/shard_map/ppermute | solution.py:55
  258.8 13.5 %collective-permute-start.7 = (bf16[2,128,768]{2,1,0:T(8,128)(2,1)}, bf16[2,128,768]{2,1,0:T(8,128)(2,1)}, u32[]{:S(2)}, u32[]{:S(2)}) collective-permute-start(bf16[2,128,768]{2,1,0:T(8,128)(2,1)} %bitcast.32), channel_id=1, source_target_pairs={{0,2},{2,4},{4,6},{1,3},{3,5},{5,7},{8,10},{10,12},{12,14},{9,11},... | collective-permute-start | bytes 1179656 | tf_op jit(solution)/shard_map/ppermute | solution.py:55
  288.2 8.8 %collective-permute-start.8 = (f32[256,768]{1,0:T(8,128)}, f32[256,768]{1,0:T(8,128)}, u32[]{:S(2)}, u32[]{:S(2)}) collective-permute-start(f32[256,768]{1,0:T(8,128)} %fusion.71), channel_id=1, source_target_pairs={{0,1},{1,0},{2,3},{3,2},{4,5},{5,4},{6,7},{7,6},{8,9},{9,8},{10,11... | collective-permute-start | bytes 2359304 | tf_op jit(solution)/shard_map/ppermute | solution.py:49
  309.5 4.4 collective-permute-start.10
  313.6 2.8 collective-permute-start.9
  341.4 14.5 %collective-permute-start.11 = (bf16[2,128,768]{2,1,0:T(8,128)(2,1)}, bf16[2,128,768]{2,1,0:T(8,128)(2,1)}, u32[]{:S(2)}, u32[]{:S(2)}) collective-permute-start(bf16[2,128,768]{2,1,0:T(8,128)(2,1)} %get-tuple-element.106), channel_id=1, source_target_pairs={{2,0},{4,2},{6,4},{3,1},{5,3},{7,5},{10,8},{12,10},{14,12},{11,9},... | collective-permute-start | bytes 1179656 | tf_op jit(solution)/shard_map/ppermute | solution.py:60
  342.7 16.2 %collective-permute-start.12 = (bf16[2,128,768]{2,1,0:T(8,128)(2,1)}, bf16[2,128,768]{2,1,0:T(8,128)(2,1)}, u32[]{:S(2)}, u32[]{:S(2)}) collective-permute-start(bf16[2,128,768]{2,1,0:T(8,128)(2,1)} %get-tuple-element.107), channel_id=1, source_target_pairs={{4,0},{6,2},{5,1},{7,3},{12,8},{14,10},{13,9},{15,11},{20,16},{22,... | collective-permute-start | bytes 1179656 | tf_op jit(solution)/shard_map/ppermute | solution.py:60
  363.7 2.0 collective-permute-start.13
  375.3 2.1 collective-permute-start.14
  376.9 157.4 %reduce-scatter.5.cloned.1.call-start = ((), (), s32[]{:S(2)}) async-start(), calls=%async_computation.8 | async-start | bytes 2506752 | tf_op jit(solution)/shard_map/reduce_scatter | solution.py:216
  398.7 19.9 %collective-permute-start.15 = (bf16[2,128,768]{2,1,0:T(8,128)(2,1)}, bf16[2,128,768]{2,1,0:T(8,128)(2,1)}, u32[]{:S(2)}, u32[]{:S(2)}) collective-permute-start(bf16[2,128,768]{2,1,0:T(8,128)(2,1)} %get-tuple-element.104), channel_id=1, source_target_pairs={{2,0},{4,2},{6,4},{3,1},{5,3},{7,5},{10,8},{12,10},{14,12},{11,9},... | collective-permute-start | bytes 1179656 | tf_op jit(solution)/shard_map/ppermute | solution.py:60
  400.0 21.9 %collective-permute-start.16 = (bf16[2,128,768]{2,1,0:T(8,128)(2,1)}, bf16[2,128,768]{2,1,0:T(8,128)(2,1)}, u32[]{:S(2)}, u32[]{:S(2)}) collective-permute-start(bf16[2,128,768]{2,1,0:T(8,128)(2,1)} %get-tuple-element.105), channel_id=1, source_target_pairs={{4,0},{6,2},{5,1},{7,3},{12,8},{14,10},{13,9},{15,11},{20,16},{22,... | collective-permute-start | bytes 1179656 | tf_op jit(solution)/shard_map/ppermute | solution.py:60
  426.4 188.9 %reduce-scatter.11.cloned.1.call-start = ((), (), s32[]{:S(2)}) async-start(), calls=%async_computation.11 | async-start | bytes 5013504 | tf_op jit(solution)/shard_map/reduce_scatter | solution.py:216
  433.4 262.9 %reduce-scatter.9.cloned.1.call-start = ((), (), s32[]{:S(2)}) async-start(), calls=%async_computation.10 | async-start | bytes 5013504 | tf_op jit(solution)/shard_map/reduce_scatter | solution.py:216
  448.5 6.8 collective-permute-start.17
  457.8 12.8 %all-to-all-start.3 = ((f32[16,8,128]{2,1,0:T(8,128)}), f32[16,8,128]{2,1,0:T(8,128)S(1)}, u32[]{:S(2)}, u32[]{:S(2)}) async-start(f32[16,8,128]{2,1,0:T(8,128)} %bitcast.125), calls=%async_computation.5 | async-start | bytes 131072 | tf_op jit(solution)/shard_map/all_to_all | solution.py:317
  470.6 11.0 %collective-permute-start.24 = (f32[8,128]{1,0:T(8,128)S(1)}, f32[8,128]{1,0:T(8,128)S(1)}, u32[]{:S(2)}, u32[]{:S(2)}) collective-permute-start(f32[8,128]{1,0:T(8,128)S(1)} %reduce_sum.395), channel_id=1, source_target_pairs={{0,2},{2,4},{4,6},{6,0},{1,3},{3,5},{5,7},{7,1},{8,10},{10,12},{12... | collective-permute-start | bytes 12296 | tf_op jit(solution)/shard_map/ppermute | solution.py:67
  477.7 5.1 collective-permute-start.25
  477.7 5.1 collective-permute-start.26
  482.9 7.7 %collective-permute-start.21 = (bf16[48,1536]{1,0:T(8,128)(2,1)}, bf16[48,1536]{1,0:T(8,128)(2,1)S(1)}, u32[]{:S(2)}, u32[]{:S(2)}) collective-permute-start(bf16[48,1536]{1,0:T(8,128)(2,1)} %reduce-scatter.7.cloned.1.call-done), channel_id=1, source_target_pairs={{0,2},{2,4},{4,6},{6,0},{1,3},{3,5},{5,7},{7,1},{8,10},{10,12},{12... | collective-permute-start | bytes 442376 | tf_op jit(solution)/shard_map/ppermute | solution.py:67
  483.0 8.8 %collective-permute-start.22 = (bf16[48,1536]{1,0:T(8,128)(2,1)}, bf16[48,1536]{1,0:T(8,128)(2,1)S(1)}, u32[]{:S(2)}, u32[]{:S(2)}) collective-permute-start(bf16[48,1536]{1,0:T(8,128)(2,1)} %reduce-scatter.7.cloned.1.call-done), channel_id=1, source_target_pairs={{0,4},{2,6},{4,0},{6,2},{1,5},{3,7},{5,1},{7,3},{8,12},{10,14},{12... | collective-permute-start | bytes 442376 | tf_op jit(solution)/shard_map/ppermute | solution.py:67
  486.9 5.4 collective-permute-start.23
  534.3 7.9 %collective-permute-start.18 = (bf16[48,1536]{1,0:T(8,128)(2,1)}, bf16[48,1536]{1,0:T(8,128)(2,1)S(1)}, u32[]{:S(2)}, u32[]{:S(2)}) collective-permute-start(bf16[48,1536]{1,0:T(8,128)(2,1)} %reduce-scatter.5.cloned.1.call-done), channel_id=1, source_target_pairs={{0,2},{2,4},{4,6},{6,0},{1,3},{3,5},{5,7},{7,1},{8,10},{10,12},{12... | collective-permute-start | bytes 442376 | tf_op jit(solution)/shard_map/ppermute | solution.py:67
  535.8 8.0 %collective-permute-start.19 = (bf16[48,1536]{1,0:T(8,128)(2,1)}, bf16[48,1536]{1,0:T(8,128)(2,1)S(1)}, u32[]{:S(2)}, u32[]{:S(2)}) collective-permute-start(bf16[48,1536]{1,0:T(8,128)(2,1)} %reduce-scatter.5.cloned.1.call-done), channel_id=1, source_target_pairs={{0,4},{2,6},{4,0},{6,2},{1,5},{3,7},{5,1},{7,3},{8,12},{10,14},{12... | collective-permute-start | bytes 442376 | tf_op jit(solution)/shard_map/ppermute | solution.py:67
  538.5 5.4 collective-permute-start.20
  615.3 10.4 %collective-permute-start.30 = (bf16[48,3072]{1,0:T(8,128)(2,1)}, bf16[48,3072]{1,0:T(8,128)(2,1)S(1)}, u32[]{:S(2)}, u32[]{:S(2)}) collective-permute-start(bf16[48,3072]{1,0:T(8,128)(2,1)} %reduce-scatter.11.cloned.1.call-done), channel_id=1, source_target_pairs={{0,2},{2,4},{4,6},{6,0},{1,3},{3,5},{5,7},{7,1},{8,10},{10,12},{12... | collective-permute-start | bytes 884744 | tf_op jit(solution)/shard_map/ppermute | solution.py:67
  616.6 14.4 %collective-permute-start.31 = (bf16[48,3072]{1,0:T(8,128)(2,1)}, bf16[48,3072]{1,0:T(8,128)(2,1)S(1)}, u32[]{:S(2)}, u32[]{:S(2)}) collective-permute-start(bf16[48,3072]{1,0:T(8,128)(2,1)} %reduce-scatter.11.cloned.1.call-done), channel_id=1, source_target_pairs={{0,4},{2,6},{4,0},{6,2},{1,5},{3,7},{5,1},{7,3},{8,12},{10,14},{12... | collective-permute-start | bytes 884744 | tf_op jit(solution)/shard_map/ppermute | solution.py:67
  619.5 11.6 %collective-permute-start.32 = (bf16[48,3072]{1,0:T(8,128)(2,1)}, bf16[48,3072]{1,0:T(8,128)(2,1)S(1)}, u32[]{:S(2)}, u32[]{:S(2)}) collective-permute-start(bf16[48,3072]{1,0:T(8,128)(2,1)} %reduce-scatter.11.cloned.1.call-done), channel_id=1, source_target_pairs={{0,6},{2,0},{4,2},{6,4},{1,7},{3,1},{5,3},{7,5},{8,14},{10,8},{12,... | collective-permute-start | bytes 884744 | tf_op jit(solution)/shard_map/ppermute | solution.py:67
  696.3 10.4 %collective-permute-start.27 = (bf16[48,3072]{1,0:T(8,128)(2,1)}, bf16[48,3072]{1,0:T(8,128)(2,1)S(1)}, u32[]{:S(2)}, u32[]{:S(2)}) collective-permute-start(bf16[48,3072]{1,0:T(8,128)(2,1)} %reduce-scatter.9.cloned.1.call-done), channel_id=1, source_target_pairs={{0,2},{2,4},{4,6},{6,0},{1,3},{3,5},{5,7},{7,1},{8,10},{10,12},{12... | collective-permute-start | bytes 884744 | tf_op jit(solution)/shard_map/ppermute | solution.py:67
  697.6 14.4 %collective-permute-start.28 = (bf16[48,3072]{1,0:T(8,128)(2,1)}, bf16[48,3072]{1,0:T(8,128)(2,1)S(1)}, u32[]{:S(2)}, u32[]{:S(2)}) collective-permute-start(bf16[48,3072]{1,0:T(8,128)(2,1)} %reduce-scatter.9.cloned.1.call-done), channel_id=1, source_target_pairs={{0,4},{2,6},{4,0},{6,2},{1,5},{3,7},{5,1},{7,3},{8,12},{10,14},{12... | collective-permute-start | bytes 884744 | tf_op jit(solution)/shard_map/ppermute | solution.py:67
  700.4 11.6 %collective-permute-start.29 = (bf16[48,3072]{1,0:T(8,128)(2,1)}, bf16[48,3072]{1,0:T(8,128)(2,1)S(1)}, u32[]{:S(2)}, u32[]{:S(2)}) collective-permute-start(bf16[48,3072]{1,0:T(8,128)(2,1)} %reduce-scatter.9.cloned.1.call-done), channel_id=1, source_target_pairs={{0,6},{2,0},{4,2},{6,4},{1,7},{3,1},{5,3},{7,5},{8,14},{10,8},{12,... | collective-permute-start | bytes 884744 | tf_op jit(solution)/shard_map/ppermute | solution.py:67
  (102 other events, 577.3 us)
Sparse Core Ops, SparseCore 0:
  377.0 79.6 reduce-scatter.6
  460.0 74.2 reduce-scatter.4
  537.6 77.6 reduce-scatter.10
  618.5 77.7 reduce-scatter.8
